TPU v7x, 32 devices: a whole 2x2x4 slice. The times are simulated.
32 devices in a mesh: leaf: 8 (over z, x), sub: 4 (over y, core).
Axes of the slice: x: 2, y: 2, z: 4, core: 2. Of those that a mesh axis runs over, the one named last changes fastest.
Arguments:
- points: float32 [65536, 64], P(('leaf', 'sub')), may hold values from -6 to 6
- leaf_maps: float32 [128, 128, 512], P(('leaf', 'sub')), may hold values from -0.25 to 0.25
- root_maps: float32 [128, 128, 512], P(('leaf', 'sub')), may hold values from -0.25 to 0.25
- current: float32 [65536], P(('leaf', 'sub')), may hold values from -6 to 6
- krylov_basis: float32 [8, 65536], P(None, ('leaf', 'sub')), may hold values from -0.0234375 to 0.0234375
- ritz_roots: float32 [2], replicated, may hold values from 40 to 400
- point_order: int32 [65536], P(('leaf', 'sub')), may hold values from 0 to 8191, as said below
- skeleton: int32 [128, 128], P(('leaf', 'sub')), may hold values from 0 to 511, as said below
- root_skeleton: int32 [8, 128], P('leaf'), may hold values from 0 to 8191, as said below
- near_list: int32 [128, 32], P(('leaf', 'sub')), may hold values from 0 to 47, as said below
- far_list: int32 [128, 4], P(('leaf', 'sub')), may hold values from 0 to 47, as said below
Outputs:
- orthogonal: float32 [65536], P(('leaf', 'sub'))
- hessenberg: float32 [9], replicated
Inputs may be any that keep to these rules, and one draw needn't show every extreme that they name: Within each subtree (block of 8192 tree positions) point_order is a permutation of 0 to 8191. `skeleton`: each row holds 128 different point numbers of the leaf. `root_skeleton`: each row holds 128 different point numbers of the subtree. `near_list`: slots count 16 leaves of the previous subtree, then the own subtree, then the next one (circularly). The first slot of leaf a is its own, 16 + (a mod 16); the slots of a row are different, and no slot of a row is in the leaf's far_list. `far_list`: slots as in near_list; different within a row, never the leaf's own.
All inputs are finite; a program needn't handle non-finite values.
Results may differ from a plain program's by a relative error of at most 0.000096.
Values sent between devices are 32-bit elements; how exact they have to be, the bound alone decides.
A program may use at most 64 MiB of HBM per device.

v0:
```python
import jax
import jax.numpy as jnp
from jax import lax
from jax.sharding import PartitionSpec as P

HIGHEST_PREC = lax.Precision.HIGHEST
RIDGE_SHIFT = 1.0
EPSILON = 1e-06


def with_halo(block, sides, width):
    for axis, dim in sides:
        count = lax.axis_size(axis)
        forward = [(i, i + 1) for i in range(count - 1)]
        forward.append((count - 1, 0))
        backward = [(target, source) for source, target in forward]
        low = lax.ppermute(
            lax.slice_in_dim(block, block.shape[dim] - width, None, axis=dim), axis, forward
        )
        high = lax.ppermute(lax.slice_in_dim(block, 0, width, axis=dim), axis, backward)
        block = jnp.concatenate([low, block, high], axis=dim)
    return block


def gaussian(inner_prod, target_sq, source_sq, feat_count):
    return jnp.exp(-(target_sq + source_sq - 2.0 * inner_prod) / feat_count)


def shards(
    points,
    leaf_maps,
    root_maps,
    current,
    krylov_basis,
    ritz_roots,
    point_order,
    skeleton,
    root_skeleton,
    near_list,
    far_list,
):
    per_device, skel_count, leaf_size = leaf_maps.shape
    feat_count = points.shape[1]
    sub_count = lax.axis_size("sub")
    sub_leaves = per_device * sub_count
    leaf_count = lax.axis_size("leaf")
    leaf_index = lax.axis_index("leaf")
    own_points = points.reshape(per_device, leaf_size, feat_count)
    own_sq = jnp.sum(own_points * own_points, axis=-1)
    skel_points = jnp.take_along_axis(own_points, skeleton[:, :, None], axis=1)
    skel_sq = jnp.sum(skel_points * skel_points, axis=-1)
    leaf_data = jnp.concatenate([own_points, skel_points], axis=1)
    subtree_data = lax.all_gather(leaf_data, "sub", axis=0, tiled=True)
    window_data = with_halo(subtree_data, (("leaf", 0),), sub_leaves)
    window_points = window_data[:, :leaf_size]
    window_sq = jnp.sum(window_points * window_points, axis=-1)
    far_points = window_data[far_list][:, :, leaf_size:]
    far_inner = jnp.einsum("bmf,bjnf->bjmn", skel_points, far_points, precision=HIGHEST_PREC)
    far_kernel = gaussian(
        far_inner,
        skel_sq[:, None, :, None],
        jnp.sum(far_points * far_points, axis=-1)[:, :, None, :],
        feat_count,
    )
    subtree_points = window_points[sub_leaves : 2 * sub_leaves].reshape(
        sub_leaves * leaf_size, feat_count
    )
    own_root = jnp.take(subtree_points, root_skeleton[0], axis=0)
    all_roots = lax.all_gather(own_root[None], "leaf", axis=0, tiled=True).reshape(
        leaf_count * skel_count, feat_count
    )
    own_root_sq = jnp.sum(own_root * own_root, axis=-1)
    all_root_sq = jnp.sum(all_roots * all_roots, axis=-1)
    top_inner = jnp.dot(own_root, all_roots.T, precision=HIGHEST_PREC)
    top_kernel = gaussian(top_inner, own_root_sq[:, None], all_root_sq[None, :], feat_count)
    distance = (jnp.arange(leaf_count, dtype=jnp.int32) - leaf_index) % leaf_count
    far_mask = (distance >= 1).astype(jnp.float32)
    top_kernel = top_kernel * jnp.repeat(far_mask, skel_count)[None, :]
    near_count = near_list.shape[1]
    neighbour_pairs = near_list.reshape(per_device, near_count // 2, 2).transpose(1, 0, 2)

    def operator(vector):
        values = vector.reshape(per_device, leaf_size)
        skel_weights = jnp.einsum("bkn,bn->bk", leaf_maps, values, precision=HIGHEST_PREC)
        root_part = jnp.einsum("bkn,bn->k", root_maps, values, precision=HIGHEST_PREC)
        packed = jnp.concatenate([values, skel_weights], axis=1)
        subtree_values = lax.all_gather(packed, "sub", axis=0, tiled=True)
        window_values = with_halo(subtree_values, (("leaf", 0),), sub_leaves)
        root_total = lax.psum(root_part, "sub")
        root_weights = lax.all_gather(root_total[None], "leaf", axis=0, tiled=True)
        window_entries = window_values[:, :leaf_size]

        def near_step(running, indices):
            sources = window_points[indices]
            inner_prod = jnp.einsum("bmf,bjnf->bjmn", own_points, sources, precision=HIGHEST_PREC)
            kernel = gaussian(
                inner_prod, own_sq[:, None, :, None], window_sq[indices][:, :, None, :], feat_count
            )
            return (
                running
                + jnp.einsum(
                    "bjmn,bjn->bm", kernel, window_entries[indices], precision=HIGHEST_PREC
                ),
                None,
            )

        start_sum = jnp.zeros((per_device, leaf_size), jnp.float32)
        result, leftover = lax.scan(near_step, start_sum, neighbour_pairs)
        skel_out = jnp.einsum(
            "bjmn,bjn->bm",
            far_kernel,
            window_values[far_list][:, :, leaf_size:],
            precision=HIGHEST_PREC,
        )
        result = result + jnp.einsum("bkn,bk->bn", leaf_maps, skel_out, precision=HIGHEST_PREC)
        root_out = jnp.dot(top_kernel, root_weights.reshape(-1), precision=HIGHEST_PREC)
        result = result + jnp.einsum("bkn,k->bn", root_maps, root_out, precision=HIGHEST_PREC)
        return result.reshape(-1) + RIDGE_SHIFT * vector

    user_subtree = lax.all_gather(current, "sub", axis=0, tiled=True)
    tree_vector = jnp.take(user_subtree, point_order, axis=0)
    first_section = tree_vector - operator(tree_vector) / ritz_roots[0]
    second = first_section - operator(first_section) / ritz_roots[1]
    preconditioned = tree_vector - second
    placed = jnp.zeros((sub_leaves * leaf_size,), jnp.float32).at[point_order].set(preconditioned)
    user_grown = lax.psum_scatter(placed, "sub", scatter_dimension=0, tiled=True)
    local_proj = jnp.dot(krylov_basis, user_grown, precision=HIGHEST_PREC)
    local_gram = jnp.dot(krylov_basis, krylov_basis.T, precision=HIGHEST_PREC)
    projections, squares, gram_matrix = lax.psum(
        (local_proj, jnp.sum(user_grown * user_grown), local_gram), ("leaf", "sub")
    )
    orthogonal = user_grown - jnp.dot(projections, krylov_basis, precision=HIGHEST_PREC)
    length_sq = (
        squares
        - 2.0 * jnp.dot(projections, projections, precision=HIGHEST_PREC)
        + jnp.dot(
            projections,
            jnp.dot(gram_matrix, projections, precision=HIGHEST_PREC),
            precision=HIGHEST_PREC,
        )
    )
    length_norm = jnp.sqrt(length_sq + EPSILON)
    return (orthogonal, jnp.concatenate([projections, length_norm[None]]))


def solution(mesh):
    return jax.shard_map(
        shards,
        mesh=mesh,
        in_specs=(
            P(("leaf", "sub"), None),
            P(("leaf", "sub"), None, None),
            P(("leaf", "sub"), None, None),
            P(("leaf", "sub")),
            P(None, ("leaf", "sub")),
            P(),
            P(("leaf", "sub")),
            P(("leaf", "sub"), None),
            P("leaf", None),
            P(("leaf", "sub"), None),
            P(("leaf", "sub"), None),
        ),
        out_specs=(P(("leaf", "sub")), P()),
        check_vma=False,
    )
```

profile of v0, /device:TPU:12, one launch (start us, length us, event | category | flops | bytes accessed | tf_op | source)
XLA Modules:
  0.0 1049.2 jit_solution(15916338392850489921)
XLA Ops:
  23.7 11.8 %gather_fusion.6 = f32[2048]{0:T(1024)S(1)} fusion(f32[8192]{0:T(1024)S(1)} %all_gather.21, s32[2048]{0:T(1024)S(1)} %get-tuple-element.217), kind=kCustom, calls=%fused_computation.6 | custom fusion | bytes 24576 | tf_op jit(solution)/shard_map/jit(_take)/gather | solution.py:121
  53.0 6.4 psum.35
  59.4 114.5 %all-gather.1 = f32[8,1,128]{2,1,0:T(1,128)S(1)} all-gather(f32[1,1,128]{2,1,0:T(1,128)S(1)} %bitcast.278), channel_id=1, replica_groups=mesh['leaf'=8,'sub'=4] {'leaf'}, dimensions={0}, use_global_device_ids=true | all-gather | bytes 4608 | tf_op jit(solution)/shard_map/all_gather | solution.py:90
  184.5 31.1 %all_gather.24 = f32[8,128,64]{1,2,0:T(8,128)S(1)} all-gather(f32[1,128,64]{1,2,0:T(8,128)S(1)} %copy.50), channel_id=1, replica_groups=mesh['leaf'=8,'sub'=4] {'leaf'}, dimensions={0}, use_global_device_ids=true | all-gather | bytes 294912 | tf_op jit(solution)/shard_map/all_gather | solution.py:69
  232.8 7.0 fusion.65
  246.3 9.7 copy.46
  256.0 337.2 %while.22 = (s32[]{:T(128)}, f32[4,512]{1,0:T(4,128)S(1)}, f32[4,512]{1,0:T(4,128)S(1)}, s32[16,4,2]{1,2,0:T(2,128)S(1)}, f32[48,512]{1,0:T(8,128)S(1)}, /*index...) while((s32[]{:T(128)}, f32[4,512]{1,0:T(4,128)S(1)}, ...), condition=%wide.region_3.4_spmd.clone, body=%wide.region_2.3_spmd.clone.sunk | while | flops 1646269440 | bytes 20656568 | solution.py:108
  262.6 8.1 fusion.120
  283.7 8.1 fusion.120
  291.8 6.3 fusion.121
  304.8 8.1 fusion.120
  325.9 8.1 fusion.120
  334.0 6.3 fusion.121
  346.9 8.1 fusion.120
  355.1 6.3 fusion.121
  368.0 8.1 fusion.120
  389.1 8.1 fusion.120
  397.2 6.3 fusion.121
  410.2 8.1 fusion.120
  431.2 8.1 fusion.120
  452.3 8.1 fusion.120
  473.4 8.1 fusion.120
  494.5 8.1 fusion.120
  515.5 8.1 fusion.120
  536.6 8.1 fusion.120
  557.7 8.1 fusion.120
  578.8 8.1 fusion.120
  610.2 19.0 %all-gather.3 = f32[8,1,128]{2,1,0:T(1,128)S(1)} all-gather(f32[1,1,128]{2,1,0:T(1,128)S(1)} %bitcast.279), channel_id=1, replica_groups=mesh['leaf'=8,'sub'=4] {'leaf'}, dimensions={0}, use_global_device_ids=true | all-gather | bytes 4608 | tf_op jit(solution)/shard_map/all_gather | solution.py:90
  635.2 337.5 %while.23 = (s32[]{:T(128)}, f32[4,512]{1,0:T(4,128)S(1)}, f32[4,512]{1,0:T(4,128)S(1)}, s32[16,4,2]{1,2,0:T(2,128)S(1)}, f32[48,512]{1,0:T(8,128)S(1)}, /*index...) while((s32[]{:T(128)}, f32[4,512]{1,0:T(4,128)S(1)}, ...), condition=%wide.region_10.11_spmd.clone, body=%wide.region_9.10_spmd.clone.sunk | while | flops 1646269440 | bytes 20656568 | solution.py:108
  642.1 8.1 fusion.126
  663.2 8.1 fusion.126
  684.3 8.1 fusion.126
  705.3 8.1 fusion.126
  726.4 8.1 fusion.126
  747.5 8.1 fusion.126
  768.6 8.1 fusion.126
  789.6 8.1 fusion.126
  810.7 8.1 fusion.126
  831.8 8.1 fusion.126
  852.9 8.1 fusion.126
  873.9 8.1 fusion.126
  895.0 8.1 fusion.126
  916.1 8.1 fusion.126
  937.2 8.1 fusion.126
  958.2 8.1 fusion.126
  974.6 8.1 scatter_custom_fusion
  982.7 10.3 all-reduce
  993.8 43.3 %all-reduce.1 = (f32[8]{0:T(128)S(1)}, f32[]{:T(128)}, f32[8,8]{1,0:T(8,128)S(1)}) all-reduce(f32[8]{0:T(128)S(1)} %convolution_bitcast_fusion.5, f32[]{:T(128)} %get-tuple-element.209, f32[8,8]{1,0:T(8,128)S(1)} %fusion.72), channel_id=1, replica_groups=mesh['leaf'=8,'sub'=4] {'leaf','sub'}, use_global_device_ids=true, to_apply=%region_14.15 | all-reduce | flops 73 | bytes 584 | tf_op jit(solution)/shard_map/psum | solution.py:129
  (483 shorter events, 483.1 us)
Async XLA Ops:
  7.2 28.4 %copy-start = (f32[4,128,512]{2,1,0:T(8,128)S(1)}, f32[4,128,512]{2,1,0:T(8,128)}, u32[]{:S(2)}) copy-start(f32[4,128,512]{2,1,0:T(8,128)} %param.16) | copy-start | bytes 3145732
  7.2 11.3 %copy-start.10 = (f32[2048]{0:T(1024)S(1)}, f32[2048]{0:T(1024)}, u32[]{:S(2)}) copy-start(f32[2048]{0:T(1024)} %param.18) | copy-start | bytes 24580
  7.2 16.5 %copy-start.9 = (s32[2048]{0:T(1024)S(1)}, s32[2048]{0:T(1024)}, u32[]{:S(2)}) copy-start(s32[2048]{0:T(1024)} %param.21) | copy-start | bytes 24580
  7.2 37.8 %all-gather.6.cloned.1.call-start = ((), (), s32[]{:S(2)}) async-start(), calls=%async_computation | async-start | bytes 3276800 | tf_op jit(solution)/shard_map/all_gather | solution.py:53
  13.7 30.4 %copy-start.12 = (s32[4,4]{1,0:T(4,128)S(1)}, s32[4,4]{1,0:T(4,128)}, u32[]{:S(2)}) copy-start(s32[4,4]{1,0:T(4,128)} %param.25) | copy-start | bytes 196
  13.8 30.5 %copy-start.13 = (f32[2]{0:T(128)S(1)}, f32[2]{0:T(128)}, u32[]{:S(2)}) copy-start(f32[2]{0:T(128)} %param.20) | copy-start | bytes 28
  13.8 31.2 %copy-start.14 = (s32[1,128]{1,0:T(1,128)S(1)}, s32[1,128]{1,0:T(1,128)}, u32[]{:S(2)}) copy-start(s32[1,128]{1,0:T(1,128)} %param.23) | copy-start | bytes 1540
  14.0 0.7 copy-start.4
  14.0 35.1 %copy-start.1 = (f32[4,128,512]{2,1,0:T(8,128)S(1)}, f32[4,128,512]{2,1,0:T(8,128)}, u32[]{:S(2)}) copy-start(f32[4,128,512]{2,1,0:T(8,128)} %param.17) | copy-start | bytes 3145732
  14.7 35.4 %copy-start.7 = (f32[8,2048]{1,0:T(8,128)S(1)}, f32[8,2048]{1,0:T(8,128)}, u32[]{:S(2)}) copy-start(f32[8,2048]{1,0:T(8,128)} %param.19) | copy-start | bytes 196612
  15.9 35.6 %copy-start.11 = (s32[4,32]{1,0:T(4,128)S(1)}, s32[4,32]{1,0:T(4,128)}, u32[]{:S(2)}) copy-start(s32[4,32]{1,0:T(4,128)} %param.24) | copy-start | bytes 1540
  15.9 35.7 %copy-start.15 = (u32[32]{0:T(128)S(1)}, u32[32]{0:T(128)}, u32[]{:S(2)}) copy-start(u32[32]{0:T(128)} %constant.135) | copy-start | bytes 388
  42.1 131.8 %collective-permute-start.3 = (f32[16,640]{1,0:T(8,128)S(1)}, f32[16,640]{1,0:T(8,128)S(1)}, u32[]{:S(2)}, u32[]{:S(2)}) collective-permute-start(f32[16,640]{1,0:T(8,128)S(1)} %reshape.306), channel_id=1, source_target_pairs={{4,0},{8,4},{12,8},{16,12},{20,16},{24,20},{28,24},{0,28},{5,1},{9... | collective-permute-start | bytes 122888 | tf_op jit(solution)/shard_map/ppermute | solution.py:20
  43.5 130.4 %collective-permute-start.2 = (f32[16,640]{1,0:T(8,128)S(1)}, f32[16,640]{1,0:T(8,128)S(1)}, u32[]{:S(2)}, u32[]{:S(2)}) collective-permute-start(f32[16,640]{1,0:T(8,128)S(1)} %reshape.306), channel_id=1, source_target_pairs={{0,4},{4,8},{8,12},{12,16},{16,20},{20,24},{24,28},{28,0},{1,5},{5... | collective-permute-start | bytes 122888 | tf_op jit(solution)/shard_map/ppermute | solution.py:17
  45.0 173.5 %collective-permute-start = (f32[16,640,64]{1,2,0:T(8,128)}, f32[16,640,64]{1,2,0:T(8,128)}, u32[]{:S(2)}, u32[]{:S(2)}) collective-permute-start(f32[16,640,64]{1,2,0:T(8,128)} %all-gather.6.cloned.1.call-done), channel_id=1, source_target_pairs={{0,4},{4,8},{8,12},{12,16},{16,20},{20,24},{24,28},{28,0},{1,5},{5... | collective-permute-start | bytes 7864328 | tf_op jit(solution)/shard_map/ppermute | solution.py:17
  48.5 175.2 %collective-permute-start.1 = (f32[16,640,64]{1,2,0:T(8,128)}, f32[16,640,64]{1,2,0:T(8,128)}, u32[]{:S(2)}, u32[]{:S(2)}) collective-permute-start(f32[16,640,64]{1,2,0:T(8,128)} %all-gather.6.cloned.1.call-done), channel_id=1, source_target_pairs={{4,0},{8,4},{12,8},{16,12},{20,16},{24,20},{28,24},{0,28},{5,1},{9... | collective-permute-start | bytes 7864328 | tf_op jit(solution)/shard_map/ppermute | solution.py:20
  174.6 47.5 %copy-start.8 = (f32[4,4,640]{2,1,0:T(4,128)}, f32[4,4,640]{2,1,0:T(4,128)S(1)}, u32[]{:S(2)}) copy-start(f32[4,4,640]{2,1,0:T(4,128)S(1)} %reshape.249) | copy-start | bytes 122884
  184.5 37.6 %copy-start.3 = (f32[16,640,64]{1,2,0:T(8,128)S(1)}, f32[16,640,64]{1,2,0:T(8,128)}, u32[]{:S(2)}) copy-start(f32[16,640,64]{1,2,0:T(8,128)} %all-gather.6.cloned.1.call-done) | copy-start | bytes 7864324
  216.6 0.8 copy-start.6
  232.8 8.1 copy-start.5
  232.8 12.2 %slice-start = ((f32[4,4,640]{2,1,0:T(4,128)}), f32[4,4,128]{2,1,0:T(4,128)S(1)}, s32[]{:S(2)}) async-start(f32[4,4,640]{2,1,0:T(4,128)} %copy-done.8), calls=%async_computation.1 | async-start | bytes 16384 | tf_op jit(solution)/shard_map/slice | solution.py:112
  244.0 1.0 copy-start.2
  602.2 30.4 %collective-permute-start.5 = (f32[16,640]{1,0:T(8,128)S(1)}, f32[16,640]{1,0:T(8,128)S(1)}, u32[]{:S(2)}, u32[]{:S(2)}) collective-permute-start(f32[16,640]{1,0:T(8,128)S(1)} %reshape.310), channel_id=1, source_target_pairs={{4,0},{8,4},{12,8},{16,12},{20,16},{24,20},{28,24},{0,28},{5,1},{9... | collective-permute-start | bytes 122888 | tf_op jit(solution)/shard_map/ppermute | solution.py:20
  602.4 30.2 %collective-permute-start.4 = (f32[16,640]{1,0:T(8,128)S(1)}, f32[16,640]{1,0:T(8,128)S(1)}, u32[]{:S(2)}, u32[]{:S(2)}) collective-permute-start(f32[16,640]{1,0:T(8,128)S(1)} %reshape.310), channel_id=1, source_target_pairs={{0,4},{4,8},{8,12},{12,16},{16,20},{20,24},{24,28},{28,0},{1,5},{5... | collective-permute-start | bytes 122888 | tf_op jit(solution)/shard_map/ppermute | solution.py:17
Sparse Core Ops, SparseCore 0:
  18.6 25.9 all-gather.5
where the time goes:
time: 1060 us; the launch traced here: 1050 us
  matrix products  479 us (45%)
  local copies, waits for them, and re-layouts  279 us (26%)
  blocking collectives  246 us (23%)
  other arithmetic  18 us (2%)
  between operations  17.6 us (2%)
    dot_general x32, matrix products, near_step(): jnp.einsum('bmf,bjnf->bjmn', own_points, sources, precision=HIGHEST_PREC)  260 us
    dot_general x32, matrix products, near_step(): jnp.einsum('bjmn,bjn->bm', kernel, window_entries[indices], precision=HIG...  200 us
    gather x32, local copies, waits for them, and re-layouts, near_step(): sources = window_points[indices]  168 us
    all_gather x2, blocking collectives, operator(): root_weights = lax.all_gather(root_total[None], 'leaf', axis=0, tiled=True)  133 us
    psum x1, blocking collectives, shards(): lax.psum((local_proj, jnp.sum(user_grown * user_grown), local_gram), ('le...  43.3 us
    all_gather x1, blocking collectives, shards(): lax.all_gather(own_root[None], 'leaf', axis=0, tiled=True)  31.1 us
  transfers between devices with their start and end apart: 7, of which 0 were waited for; matrix products, arithmetic and copies ran while one was open for 4% of the time, Pallas kernels for 0%

commit v1 on v0

--- a/solution.py
+++ b/solution.py
@@ -1,6 +1,8 @@
 import jax
 import jax.numpy as jnp
 from jax import lax
+from jax.experimental import pallas as pl
+from jax.experimental.pallas import tpu as pltpu
 from jax.sharding import PartitionSpec as P
 
 HIGHEST_PREC = lax.Precision.HIGHEST
@@ -20,6 +22,86 @@
         high = lax.ppermute(lax.slice_in_dim(block, 0, width, axis=dim), axis, backward)
         block = jnp.concatenate([low, block, high], axis=dim)
     return block
+
+
+def split3(x):
+    a = x.astype(jnp.bfloat16)
+    r = x - a.astype(jnp.float32)
+    b = r.astype(jnp.bfloat16)
+    c = (r - b.astype(jnp.float32)).astype(jnp.bfloat16)
+    return a, b, c
+
+
+def target_rows(own_points, scale):
+    x = own_points * (2.0 * scale)
+    hi = x.astype(jnp.bfloat16)
+    lo = (x - hi.astype(jnp.float32)).astype(jnp.bfloat16)
+    sq = -scale * jnp.sum(own_points * own_points, axis=-1, keepdims=True)
+    a, b, c = split3(sq)
+    one = jnp.ones_like(a)
+    feat = own_points.shape[-1]
+    pad = jnp.zeros(own_points.shape[:-1] + (feat - 6,), jnp.bfloat16)
+    return jnp.concatenate([hi, lo, hi, one, one, one, a, b, c, pad], axis=-1)
+
+
+def near_kernel(scale, near_ref, t_ref, w_ref, v_ref, out_ref, aug_ref, acc_ref):
+    window, feat, size = w_ref.shape
+    per_device = t_ref.shape[0]
+    near_count = near_ref.shape[1]
+
+    def build(i, carry):
+        x = w_ref[i]
+        hi = x.astype(jnp.bfloat16)
+        lo = (x - hi.astype(jnp.float32)).astype(jnp.bfloat16)
+        sq = -scale * jnp.sum(x * x, axis=0, keepdims=True)
+        s1 = sq.astype(jnp.bfloat16).astype(jnp.float32)
+        s2 = (sq - s1).astype(jnp.bfloat16).astype(jnp.float32)
+        s3 = sq - s1 - s2
+        row = lax.broadcasted_iota(jnp.int32, (feat, size), 0)
+        extra = jnp.where(
+            row == 0, s1, jnp.where(row == 1, s2, jnp.where(row == 2, s3, jnp.where(row < 6, 1.0, 0.0)))
+        )
+        aug_ref[i, pl.ds(0, feat)] = hi
+        aug_ref[i, pl.ds(feat, feat)] = hi
+        aug_ref[i, pl.ds(2 * feat, feat)] = lo
+        aug_ref[i, pl.ds(3 * feat, feat)] = extra.astype(jnp.bfloat16)
+        return carry
+
+    lax.fori_loop(0, window, build, 0)
+    for b in range(per_device):
+        acc_ref[...] = jnp.zeros_like(acc_ref)
+
+        def step(s, carry):
+            slot = near_ref[b, s]
+            inner = jnp.dot(t_ref[b], aug_ref[slot], preferred_element_type=jnp.float32)
+            prod = jnp.exp2(inner) * v_ref[slot]
+            total = prod[:, 0:128]
+            for g in range(1, size // 128):
+                total = total + prod[:, g * 128 : (g + 1) * 128]
+            acc_ref[...] += total
+            return carry
+
+        lax.fori_loop(0, near_count, step, 0)
+        out_ref[b] = acc_ref[...]
+
+
+def near_apply(near_list, targets, window_t, values, scale):
+    per_device, size, width = targets.shape
+    window, feat, _ = window_t.shape
+    vmem = pl.BlockSpec(memory_space=pltpu.VMEM)
+    part = pl.pallas_call(
+        lambda *refs: near_kernel(scale, *refs),
+        out_shape=jax.ShapeDtypeStruct((per_device, size, 128), jnp.float32),
+        in_specs=[pl.BlockSpec(memory_space=pltpu.SMEM), vmem, vmem, vmem],
+        out_specs=vmem,
+        scratch_shapes=[
+            pltpu.VMEM((window, width, size), jnp.bfloat16),
+            pltpu.VMEM((size, 128), jnp.float32),
+        ],
+        compiler_params=pltpu.CompilerParams(vmem_limit_bytes=48 * 1024 * 1024),
+        name="near",
+    )(near_list, targets, window_t, values)
+    return jnp.sum(part, axis=-1)
 
 
 def gaussian(inner_prod, target_sq, source_sq, feat_count):
@@ -46,15 +128,15 @@
     leaf_count = lax.axis_size("leaf")
     leaf_index = lax.axis_index("leaf")
     own_points = points.reshape(per_device, leaf_size, feat_count)
-    own_sq = jnp.sum(own_points * own_points, axis=-1)
     skel_points = jnp.take_along_axis(own_points, skeleton[:, :, None], axis=1)
     skel_sq = jnp.sum(skel_points * skel_points, axis=-1)
-    leaf_data = jnp.concatenate([own_points, skel_points], axis=1)
+    leaf_data = jnp.concatenate([own_points, skel_points], axis=1).transpose(0, 2, 1)
     subtree_data = lax.all_gather(leaf_data, "sub", axis=0, tiled=True)
     window_data = with_halo(subtree_data, (("leaf", 0),), sub_leaves)
-    window_points = window_data[:, :leaf_size]
-    window_sq = jnp.sum(window_points * window_points, axis=-1)
-    far_points = window_data[far_list][:, :, leaf_size:]
+    window_t = window_data[:, :, :leaf_size]
+    scale = 1.4426950408889634 / feat_count
+    targets = target_rows(own_points, scale)
+    far_points = window_data[:, :, leaf_size:][far_list].transpose(0, 1, 3, 2)
     far_inner = jnp.einsum("bmf,bjnf->bjmn", skel_points, far_points, precision=HIGHEST_PREC)
     far_kernel = gaussian(
         far_inner,
@@ -62,10 +144,9 @@
         jnp.sum(far_points * far_points, axis=-1)[:, :, None, :],
         feat_count,
     )
-    subtree_points = window_points[sub_leaves : 2 * sub_leaves].reshape(
-        sub_leaves * leaf_size, feat_count
-    )
-    own_root = jnp.take(subtree_points, root_skeleton[0], axis=0)
+    subtree_points = subtree_data[:, :, :leaf_size]
+    root_index = root_skeleton[0]
+    own_root = subtree_points[root_index // leaf_size, :, root_index % leaf_size]
     all_roots = lax.all_gather(own_root[None], "leaf", axis=0, tiled=True).reshape(
         leaf_count * skel_count, feat_count
     )
@@ -76,9 +157,6 @@
     distance = (jnp.arange(leaf_count, dtype=jnp.int32) - leaf_index) % leaf_count
     far_mask = (distance >= 1).astype(jnp.float32)
     top_kernel = top_kernel * jnp.repeat(far_mask, skel_count)[None, :]
-    near_count = near_list.shape[1]
-    neighbour_pairs = near_list.reshape(per_device, near_count // 2, 2).transpose(1, 0, 2)
-
     def operator(vector):
         values = vector.reshape(per_device, leaf_size)
         skel_weights = jnp.einsum("bkn,bn->bk", leaf_maps, values, precision=HIGHEST_PREC)
@@ -90,22 +168,7 @@
         root_weights = lax.all_gather(root_total[None], "leaf", axis=0, tiled=True)
         window_entries = window_values[:, :leaf_size]
 
-        def near_step(running, indices):
-            sources = window_points[indices]
-            inner_prod = jnp.einsum("bmf,bjnf->bjmn", own_points, sources, precision=HIGHEST_PREC)
-            kernel = gaussian(
-                inner_prod, own_sq[:, None, :, None], window_sq[indices][:, :, None, :], feat_count
-            )
-            return (
-                running
-                + jnp.einsum(
-                    "bjmn,bjn->bm", kernel, window_entries[indices], precision=HIGHEST_PREC
-                ),
-                None,
-            )
-
-        start_sum = jnp.zeros((per_device, leaf_size), jnp.float32)
-        result, leftover = lax.scan(near_step, start_sum, neighbour_pairs)
+        result = near_apply(near_list, targets, window_t, window_entries[:, None, :], scale)
         skel_out = jnp.einsum(
             "bjmn,bjn->bm",
             far_kernel,

time: 1060 us -> 442 us (0.42)
  matrix products: 479 us -> 17.8 us
  local copies, waits for them, and re-layouts: 279 us -> 63.9 us
  Pallas kernels: 0 us -> 88.8 us
  blocking collectives: 246 us -> 231 us
    dot_general x64 -> x0, matrix products: 460 us -> none  [the longest x32 260 us: near_step(): jnp.einsum('bmf,bjnf->bjmn', own_points, sources, precision=HIGHEST_PREC)]
    gather x162 -> x2, local copies, waits for them, and re-layouts: 214 us -> 3.77 us  [the longest x1 2 us: shards(): far_points = window_data[:, :, leaf_size:][far_list].transpose(0, 1, 3, 2)]
    pallas_call x0 -> x2, Pallas kernels: none -> 88.8 us  [near_apply(): pl.pallas_call(lambda *refs: near_kernel(scale, *refs), out_shape=jax.Sha...]
    all_gather x2, blocking collectives: 133 us -> 117 us  [operator(): root_weights = lax.all_gather(root_total[None], 'leaf', axis=0, tiled=True)]
    unnamed x47 -> x50, local copies, waits for them, and re-layouts: 20.8 us -> 8.51 us
  transfers between devices with their start and end apart: 7 -> 7, of which waited for: 0 -> 0; matrix products, arithmetic and copies ran while one was open for 4% -> 12% of each run, Pallas kernels for 0% -> 0%
where the time goes in v1:
time: 442 us; the launch traced here: 441 us
  blocking collectives  231 us (52%)
  Pallas kernels  88.8 us (20%)
  local copies, waits for them, and re-layouts  63.9 us (14%)
  matrix products  17.8 us (4%)
  between operations  17.1 us (4%)
  other arithmetic  13.4 us (3%)
  starting transfers between devices  8.96 us (2%)
    all_gather x2, blocking collectives, operator(): root_weights = lax.all_gather(root_total[None], 'leaf', axis=0, tiled=True)  117 us
    pallas_call x2, Pallas kernels, near_apply(): pl.pallas_call(lambda *refs: near_kernel(scale, *refs), out_shape=jax.Sha...  88.8 us
    psum x1, blocking collectives, shards(): lax.psum((local_proj, jnp.sum(user_grown * user_grown), local_gram), ('le...  43.4 us
    all_gather x1, blocking collectives, shards(): lax.all_gather(own_root[None], 'leaf', axis=0, tiled=True)  32 us
    psum x2, blocking collectives, operator(): root_total = lax.psum(root_part, 'sub')  11.9 us
    gather x1, local copies, waits for them, and re-layouts, shards(): tree_vector = jnp.take(user_subtree, point_order, axis=0)  11.8 us
    all_gather x2, blocking collectives, operator(): subtree_values = lax.all_gather(packed, 'sub', axis=0, tiled=True)  10.8 us
    unnamed x1, blocking collectives  10.3 us
  transfers between devices with their start and end apart: 7, of which 0 were waited for; matrix products, arithmetic and copies ran while one was open for 12% of the time, Pallas kernels for 0%

profile of v1, /device:TPU:12, one launch (start us, length us, event | category | flops | bytes accessed | tf_op | source)
XLA Modules:
  0.0 440.7 jit_solution(15291712843739102423)
XLA Ops:
  8.7 1.4 reshape.225
  10.5 3.7 gather_fusion.5
  15.1 0.9 copy.46
  16.0 5.2 %all_gather.21 = f32[8192]{0:T(1024)S(1)} all-gather(f32[2048]{0:T(1024)S(1)} %copy-done.14), channel_id=1, replica_groups=mesh['leaf'=8,'sub'=4] {'sub'}, dimensions={0}, use_global_device_ids=true | all-gather | bytes 40960 | tf_op jit(solution)/shard_map/all_gather | solution.py:183
  21.8 11.8 %gather_fusion = f32[2048]{0:T(1024)S(1)} fusion(f32[8192]{0:T(1024)S(1)} %all_gather.21, s32[2048]{0:T(1024)S(1)} %get-tuple-element.15), kind=kCustom, calls=%fused_computation | custom fusion | bytes 24576 | tf_op jit(solution)/shard_map/jit(_take)/gather | solution.py:184
  33.6 1.0 fusion.34
  34.6 5.6 %all-gather.1 = f32[4,4,640]{2,1,0:T(4,128)S(1)} all-gather(f32[1,4,640]{2,1,0:T(4,128)S(1)} %maximum_bitcast_fusion.1), channel_id=1, replica_groups=mesh['leaf'=8,'sub'=4] {'sub'}, dimensions={0}, use_global_device_ids=true | all-gather | bytes 51200 | tf_op jit(solution)/shard_map/all_gather | solution.py:165
  40.2 1.5 collective-permute-start.2
  41.7 1.4 collective-permute-start.3
  43.2 0.9 convolution_bitcast_fusion.3
  45.4 1.1 multiply_reduce_fusion.2
  46.5 2.4 collective-permute-start.1
  49.5 1.4 copy.41
  50.9 1.3 copy.42
  52.2 0.8 fusion.39
  53.1 1.2 subtract_convert_fusion.1
  54.2 2.7 subtract_convert_fusion
  56.9 1.0 copy.43
  59.1 0.9 broadcast_in_dim.60
  60.0 0.9 concatenate.30
  60.9 4.9 %concatenate.31.refs_1_ = bf16[4,512,256]{2,1,0:T(8,128)(2,1)S(1)} concatenate(bf16[4,512,64]{2,1,0:T(8,128)(2,1)} %get-tuple-element.12, bf16[4,512,64]{2,1,0:T(8,128)(2,1)} %get-tuple-element.11, bf16[4,512,64]{2,1,0:T(8,128)(2,1)} %get-tuple-element.12, bf16[4,512,3]{2,1,0:T(8,128)(2,1)} %concatenate.30, bf16[4,512,1]{2,1,0:T(8,128)(2,1)} %copy.43, ...), dimensions={2} | concatenate | bytes 2097152 | tf_op jit(solution)/shard_map/concatenate | solution.py:44
  65.8 6.1 %psum.35 = f32[1,128]{1,0:T(1,128)S(1)} all-reduce(f32[1,128]{1,0:T(1,128)S(1)} %convolution_bitcast_fusion.3), channel_id=1, replica_groups=mesh['leaf'=8,'sub'=4] {'sub'}, use_global_device_ids=true, to_apply=%region_6.7 | all-reduce | flops 128 | bytes 1024 | tf_op jit(solution)/shard_map/psum | solution.py:167
  71.9 98.6 %all-gather.2 = f32[8,1,128]{2,1,0:T(1,128)} all-gather(f32[1,1,128]{2,1,0:T(1,128)S(1)} %bitcast.197), channel_id=1, replica_groups=mesh['leaf'=8,'sub'=4] {'leaf'}, dimensions={0}, use_global_device_ids=true | all-gather | bytes 4608 | tf_op jit(solution)/shard_map/all_gather | solution.py:168
  173.3 1.0 broadcast_in_dim.63.refs_3_
  174.3 3.2 slice.52
  177.5 3.8 copy.71
  181.3 1.8 gather_fusion.3
  183.2 32.0 %all-gather = f32[1024,64]{1,0:T(8,128)S(1)} all-gather(f32[128,64]{1,0:T(8,128)S(1)} %gather_fusion.3), channel_id=2, replica_groups=mesh['leaf'=8,'sub'=4] {'leaf'}, dimensions={0}, use_global_device_ids=true | all-gather | bytes 294912 | tf_op jit(solution)/shard_map/all_gather | solution.py:150
  217.3 1.9 constant_dynamic-update-slice_fusion.2
  219.5 1.9 constant_dynamic-update-slice_fusion
  221.4 1.2 slice.50
  222.7 3.5 slice.48.refs_2_
  226.1 2.0 gather_fusion.1
  229.0 3.0 fusion.4
  233.6 44.4 %near.2 = f32[4,512,128]{2,1,0:T(8,128)S(1)} custom-call(s32[4,32]{1,0:T(4,128)S(1)} %copy-done.1, bf16[4,512,256]{2,1,0:T(8,128)(2,1)S(1)} %concatenate.31.refs_1_, f32[48,64,512]{2,1,0:T(8,128)} %slice.48.refs_2_, f32[48,1,512]{2,1,0:T(1,128)S(1)} %broadcast_in_dim.63.refs_3_), custom_call_target="tpu_custom_call" | custom-call | tf_op jit(solution)/shard_map/near/pallas_call | solution.py:92
  279.1 1.0 fusion.17
  280.1 5.2 %all-gather.3 = f32[4,4,640]{2,1,0:T(4,128)S(1)} all-gather(f32[1,4,640]{2,1,0:T(4,128)S(1)} %maximum_bitcast_fusion.2), channel_id=1, replica_groups=mesh['leaf'=8,'sub'=4] {'sub'}, dimensions={0}, use_global_device_ids=true | all-gather | bytes 51200 | tf_op jit(solution)/shard_map/all_gather | solution.py:165
  285.4 2.9 collective-permute-start.5
  288.3 2.1 convolution_bitcast_fusion.2
  290.4 5.8 %psum.36 = f32[1,128]{1,0:T(1,128)S(1)} all-reduce(f32[1,128]{1,0:T(1,128)S(1)} %convolution_bitcast_fusion.2), channel_id=1, replica_groups=mesh['leaf'=8,'sub'=4] {'sub'}, use_global_device_ids=true, to_apply=%region_8.9 | all-reduce | flops 128 | bytes 1024 | tf_op jit(solution)/shard_map/psum | solution.py:167
  296.2 18.6 %all-gather.4 = f32[8,1,128]{2,1,0:T(1,128)S(1)} all-gather(f32[1,1,128]{2,1,0:T(1,128)S(1)} %bitcast.198), channel_id=1, replica_groups=mesh['leaf'=8,'sub'=4] {'leaf'}, dimensions={0}, use_global_device_ids=true | all-gather | bytes 4608 | tf_op jit(solution)/shard_map/all_gather | solution.py:168
  314.8 1.5 convolution_bitcast_fusion.6
  316.3 1.8 fusion.38
  320.2 44.4 %near.3 = f32[4,512,128]{2,1,0:T(8,128)S(1)} custom-call(s32[4,32]{1,0:T(4,128)S(1)} %copy-done.1, bf16[4,512,256]{2,1,0:T(8,128)(2,1)S(1)} %concatenate.31.refs_1_, f32[48,64,512]{2,1,0:T(8,128)} %slice.48.refs_2_, f32[48,1,512]{2,1,0:T(1,128)S(1)} %broadcast_in_dim.68.refs_3_), custom_call_target="tpu_custom_call" | custom-call | tf_op jit(solution)/shard_map/near/pallas_call | solution.py:92
  365.1 1.3 subtract_subtract_fusion
  366.3 8.2 %scatter_custom_fusion = f32[8192]{0:T(1024)S(1)} fusion(s32[2048]{0:T(1024)} %get-tuple-element.16, f32[2048]{0:T(1024)S(1)} %subtract_subtract_fusion, f32[]{:T(128)} %constant.52.clone.1), kind=kCustom, calls=%fused_computation.51 | custom fusion | bytes 33280 | tf_op jit(solution)/shard_map/scatter | solution.py:188
  374.6 10.3 %all-reduce = f32[8192]{0:T(1024)S(1)} all-reduce(f32[8192]{0:T(1024)S(1)} %scatter_custom_fusion), channel_id=3, replica_groups=mesh['leaf'=8,'sub'=4] {'sub'}, use_global_device_ids=true, to_apply=%region_10.11.clone | all-reduce | flops 8192 | bytes 65536
  385.7 43.4 %all-reduce.1 = (f32[8]{0:T(128)S(1)}, f32[]{:T(128)}, f32[8,8]{1,0:T(8,128)S(1)}) all-reduce(f32[8]{0:T(128)S(1)} %convolution_bitcast_fusion.5, f32[]{:T(128)} %get-tuple-element.5, f32[8,8]{1,0:T(8,128)S(1)} %copy-done.12), channel_id=1, replica_groups=mesh['leaf'=8,'sub'=4] {'leaf','sub'}, use_global_device_ids=true, to_apply=%region_11.12 | all-reduce | flops 73 | bytes 584 | tf_op jit(solution)/shard_map/psum | solution.py:192
  (112 shorter events, 20.7 us)
Async XLA Ops:
  7.2 26.4 %copy-start = (f32[4,128,512]{2,1,0:T(8,128)S(1)}, f32[4,128,512]{2,1,0:T(8,128)}, u32[]{:S(2)}) copy-start(f32[4,128,512]{2,1,0:T(8,128)} %param.12) | copy-start | bytes 3145732
  7.2 37.6 %all-gather.7.cloned.1.call-start = ((), (), s32[]{:S(2)}) async-start(), calls=%async_computation | async-start | bytes 3276800 | tf_op jit(solution)/shard_map/all_gather | solution.py:134
  10.1 5.9 %copy-start.14 = (f32[2048]{0:T(1024)S(1)}, f32[2048]{0:T(1024)}, u32[]{:S(2)}) copy-start(f32[2048]{0:T(1024)} %param.14) | copy-start | bytes 24580
  10.1 11.1 %copy-start.9 = (s32[2048]{0:T(1024)S(1)}, s32[2048]{0:T(1024)}, u32[]{:S(2)}) copy-start(s32[2048]{0:T(1024)} %param.17) | copy-start | bytes 24580
  21.8 21.4 %copy-start.2 = (f32[4,128,512]{2,1,0:T(8,128)S(1)}, f32[4,128,512]{2,1,0:T(8,128)}, u32[]{:S(2)}) copy-start(f32[4,128,512]{2,1,0:T(8,128)} %param.13) | copy-start | bytes 3145732
  21.8 22.3 %copy-start.17 = (s32[1,128]{1,0:T(1,128)S(1)}, s32[1,128]{1,0:T(1,128)}, u32[]{:S(2)}) copy-start(s32[1,128]{1,0:T(1,128)} %param.19) | copy-start | bytes 1540
  21.8 22.3 %copy-start.15 = (s32[4,4]{1,0:T(4,128)S(1)}, s32[4,4]{1,0:T(4,128)}, u32[]{:S(2)}) copy-start(s32[4,4]{1,0:T(4,128)} %param.21) | copy-start | bytes 196
  21.8 27.1 %copy-start.16 = (f32[2]{0:T(128)S(1)}, f32[2]{0:T(128)}, u32[]{:S(2)}) copy-start(f32[2]{0:T(128)} %param.16) | copy-start | bytes 28
  33.6 18.7 %copy-start.8 = (f32[8,2048]{1,0:T(8,128)S(1)}, f32[8,2048]{1,0:T(8,128)}, u32[]{:S(2)}) copy-start(f32[8,2048]{1,0:T(8,128)} %param.15) | copy-start | bytes 196612
  40.2 130.4 %collective-permute-start.2 = (f32[16,640]{1,0:T(8,128)S(1)}, f32[16,640]{1,0:T(8,128)}, u32[]{:S(2)}, u32[]{:S(2)}) collective-permute-start(f32[16,640]{1,0:T(8,128)S(1)} %reshape.302), channel_id=1, source_target_pairs={{0,4},{4,8},{8,12},{12,16},{16,20},{20,24},{24,28},{28,0},{1,5},{5... | collective-permute-start | bytes 122888 | tf_op jit(solution)/shard_map/ppermute | solution.py:19
  41.7 129.6 %collective-permute-start.3 = (f32[16,640]{1,0:T(8,128)S(1)}, f32[16,640]{1,0:T(8,128)}, u32[]{:S(2)}, u32[]{:S(2)}) collective-permute-start(f32[16,640]{1,0:T(8,128)S(1)} %reshape.302), channel_id=1, source_target_pairs={{4,0},{8,4},{12,8},{16,12},{20,16},{24,20},{28,24},{0,28},{5,1},{9... | collective-permute-start | bytes 122888 | tf_op jit(solution)/shard_map/ppermute | solution.py:22
  44.8 13.2 %copy-start.18 = (u32[32]{0:T(128)S(1)}, u32[32]{0:T(128)}, u32[]{:S(2)}) copy-start(u32[32]{0:T(128)} %constant.141) | copy-start | bytes 388
  44.8 172.5 %collective-permute-start = (f32[16,64,640]{2,1,0:T(8,128)}, f32[16,64,640]{2,1,0:T(8,128)}, u32[]{:S(2)}, u32[]{:S(2)}) collective-permute-start(f32[16,64,640]{2,1,0:T(8,128)} %all-gather.7.cloned.1.call-done), channel_id=1, source_target_pairs={{0,4},{4,8},{8,12},{12,16},{16,20},{20,24},{24,28},{28,0},{1,5},{5... | collective-permute-start | bytes 7864328 | tf_op jit(solution)/shard_map/ppermute | solution.py:19
  46.5 173.0 %collective-permute-start.1 = (f32[16,64,640]{2,1,0:T(8,128)}, f32[16,64,640]{2,1,0:T(8,128)}, u32[]{:S(2)}, u32[]{:S(2)}) collective-permute-start(f32[16,64,640]{2,1,0:T(8,128)} %all-gather.7.cloned.1.call-done), channel_id=1, source_target_pairs={{4,0},{8,4},{12,8},{16,12},{20,16},{24,20},{28,24},{0,28},{5,1},{9... | collective-permute-start | bytes 7864328 | tf_op jit(solution)/shard_map/ppermute | solution.py:22
  177.5 37.9 %copy-start.10 = (f32[1024]{0:T(1024)S(1)}, f32[1024]{0:T(1024)}, u32[]{:S(2)}) copy-start(f32[1024]{0:T(1024)} %broadcast_bitcast_fusion) | copy-start | bytes 12292
  177.5 38.6 %copy-start.11 = (f32[8,1,128]{2,1,0:T(1,128)S(1)}, f32[8,1,128]{2,1,0:T(1,128)}, u32[]{:S(2)}) copy-start(f32[8,1,128]{2,1,0:T(1,128)} %all-gather.2) | copy-start | bytes 12292
  215.2 4.0 copy-start.5
  216.1 1.1 copy-start.6
  222.7 6.3 %copy-start.13 = (f32[4,128]{1,0:T(4,128)S(1)}, f32[4,128]{1,0:T(4,128)}, u32[]{:S(2)}) copy-start(f32[4,128]{1,0:T(4,128)} %get-tuple-element.7) | copy-start | bytes 6148
  226.1 7.5 %copy-start.1 = (s32[4,32]{1,0:T(4,128)S(1)}, s32[4,32]{1,0:T(4,128)}, u32[]{:S(2)}) copy-start(s32[4,32]{1,0:T(4,128)} %refs_0_.3) | copy-start | bytes 1540
  228.1 0.8 copy-start.7
  232.0 1.0 copy-start.3
  278.3 40.5 %copy-start.4 = (f32[4,4,128,128]{2,3,1,0:T(8,128)S(1)}, f32[4,4,128,128]{2,3,1,0:T(8,128)}, u32[]{:S(2)}) copy-start(f32[4,4,128,128]{2,3,1,0:T(8,128)} %copy-done.3) | copy-start | bytes 3145732
  285.3 32.9 %collective-permute-start.4 = (f32[16,640]{1,0:T(8,128)S(1)}, f32[16,640]{1,0:T(8,128)S(1)}, u32[]{:S(2)}, u32[]{:S(2)}) collective-permute-start(f32[16,640]{1,0:T(8,128)S(1)} %reshape.306), channel_id=1, source_target_pairs={{0,4},{4,8},{8,12},{12,16},{16,20},{20,24},{24,28},{28,0},{1,5},{5... | collective-permute-start | bytes 122888 | tf_op jit(solution)/shard_map/ppermute | solution.py:19
  285.4 32.8 %collective-permute-start.5 = (f32[16,640]{1,0:T(8,128)S(1)}, f32[16,640]{1,0:T(8,128)S(1)}, u32[]{:S(2)}, u32[]{:S(2)}) collective-permute-start(f32[16,640]{1,0:T(8,128)S(1)} %reshape.306), channel_id=1, source_target_pairs={{4,0},{8,4},{12,8},{16,12},{20,16},{24,20},{28,24},{0,28},{5,1},{9... | collective-permute-start | bytes 122888 | tf_op jit(solution)/shard_map/ppermute | solution.py:22
  320.2 65.4 %copy-start.12 = (f32[8,8]{1,0:T(8,128)S(1)}, f32[8,8]{1,0:T(8,128)}, u32[]{:S(2)}) copy-start(f32[8,8]{1,0:T(8,128)} %fusion.39) | copy-start | bytes 772
Sparse Core Ops, SparseCore 0:
  16.1 25.9 all-gather.6

commit v2 on v1

--- a/solution.py
+++ b/solution.py
@@ -10,18 +10,215 @@
 EPSILON = 1e-06
 
 
-def with_halo(block, sides, width):
-    for axis, dim in sides:
-        count = lax.axis_size(axis)
-        forward = [(i, i + 1) for i in range(count - 1)]
-        forward.append((count - 1, 0))
-        backward = [(target, source) for source, target in forward]
-        low = lax.ppermute(
-            lax.slice_in_dim(block, block.shape[dim] - width, None, axis=dim), axis, forward
-        )
-        high = lax.ppermute(lax.slice_in_dim(block, 0, width, axis=dim), axis, backward)
-        block = jnp.concatenate([low, block, high], axis=dim)
-    return block
+MESH = pl.DeviceIdType.MESH
+VMEM = pl.BlockSpec(memory_space=pltpu.VMEM)
+
+
+def position():
+    return (
+        lax.axis_index("leaf"),
+        lax.axis_index("sub"),
+        lax.axis_size("leaf"),
+        lax.axis_size("sub"),
+    )
+
+
+def greet(peers):
+    leaf, sub, leaf_count, sub_count = position()
+    barrier = pltpu.get_barrier_semaphore()
+    for dl, ds in peers:
+        there = (lax.rem(leaf + dl, leaf_count), lax.rem(sub + ds, sub_count))
+        pl.semaphore_signal(barrier, inc=1, device_id=there, device_id_type=MESH)
+    pl.semaphore_wait(barrier, len(peers))
+
+
+class Channel:
+    def __init__(self, block, lead, peers, slot, per_target=False):
+        self.block, self.peers, self.slot, self.per_target = block, peers, slot, per_target
+        shape = block.shape[1:] if per_target else block.shape
+        self.out = jax.ShapeDtypeStruct(tuple(lead) + shape, block.dtype)
+
+
+def exchange(channels, collective_id):
+    count = len(channels)
+    greeted = sorted({peer for channel in channels for peer in channel.peers})
+
+    def kernel(*refs):
+        leaf, sub, leaf_count, sub_count = position()
+        ins, outs = refs[:count], refs[count : 2 * count]
+        sems = refs[2 * count :]
+        greet(greeted)
+        started = []
+        for c, channel in enumerate(channels):
+            send, recv = sems[2 * c], sems[2 * c + 1]
+            for k, (dl, ds) in enumerate(channel.peers):
+                there = (lax.rem(leaf + dl, leaf_count), lax.rem(sub + ds, sub_count))
+                source = ins[c].at[there[1]] if channel.per_target else ins[c]
+                copy = pltpu.make_async_remote_copy(
+                    src_ref=source,
+                    dst_ref=outs[c].at[channel.slot(leaf, sub, dl, sub_count)],
+                    send_sem=send.at[k],
+                    recv_sem=recv.at[k],
+                    device_id=there,
+                    device_id_type=MESH,
+                )
+                copy.start()
+                started.append(copy)
+        for c, channel in enumerate(channels):
+            own = ins[c][sub] if channel.per_target else ins[c][...]
+            outs[c][channel.slot(leaf, sub, 0, sub_count)] = own
+        for copy in started:
+            copy.wait_send()
+        for c, channel in enumerate(channels):
+            send, recv = sems[2 * c], sems[2 * c + 1]
+            for k, (dl, ds) in enumerate(channel.peers):
+                here = (
+                    lax.rem(leaf + leaf_count - dl, leaf_count),
+                    lax.rem(sub + sub_count - ds, sub_count),
+                )
+                slot = channel.slot(here[0], here[1], dl, sub_count)
+                pltpu.make_async_remote_copy(
+                    src_ref=outs[c].at[slot],
+                    dst_ref=outs[c].at[slot],
+                    send_sem=send.at[k],
+                    recv_sem=recv.at[k],
+                    device_id=here,
+                    device_id_type=MESH,
+                ).wait_recv()
+
+    scratch = []
+    for channel in channels:
+        scratch += [pltpu.SemaphoreType.DMA((len(channel.peers),))] * 2
+    return pl.pallas_call(
+        kernel,
+        out_shape=[channel.out for channel in channels],
+        in_specs=[VMEM] * count,
+        out_specs=[VMEM] * count,
+        scratch_shapes=scratch,
+        compiler_params=pltpu.CompilerParams(collective_id=collective_id, has_side_effects=True),
+        name="exchange",
+    )(*[channel.block for channel in channels])
+
+
+def sub_peers():
+    return [(0, ds) for ds in range(1, lax.axis_size("sub"))]
+
+
+def leaf_peers():
+    return [(dl, 0) for dl in range(1, lax.axis_size("leaf"))]
+
+
+def all_peers():
+    subs = lax.axis_size("sub")
+    return [(dl, ds) for dl in range(lax.axis_size("leaf")) for ds in range(subs) if dl or ds]
+
+
+def window_peers():
+    subs, leaves = lax.axis_size("sub"), lax.axis_size("leaf")
+    return [(dl, ds) for dl in (0, 1, leaves - 1) for ds in range(subs) if dl or ds]
+
+
+def sub_slot(leaf, sub, dl, sub_count):
+    return sub
+
+
+def leaf_slot(leaf, sub, dl, sub_count):
+    return leaf
+
+
+def all_slot(leaf, sub, dl, sub_count):
+    return leaf * sub_count + sub
+
+
+def window_slot(leaf, sub, dl, sub_count):
+    part = 1 if dl == 0 else (0 if dl == 1 else 2)
+    return part * sub_count + sub
+
+
+def gather_window(block, collective_id):
+    subs, leaves = lax.axis_size("sub"), lax.axis_size("leaf")
+    chips = subs // 2
+    hops = [(1, 0), (leaves - 1, 0)]
+
+    def kernel(x_ref, out_ref, halo_send, recv, chip_send, core_send):
+        leaf, sub, leaf_count, sub_count = position()
+        chip, core = sub // 2, lax.rem(sub, 2)
+        other = chip * 2 + 1 - core
+        greet([(0, ds) for ds in range(1, subs)] + hops)
+
+        def remote(source, part, owner, send, there):
+            return pltpu.make_async_remote_copy(
+                src_ref=source,
+                dst_ref=out_ref.at[part * sub_count + owner],
+                send_sem=send,
+                recv_sem=recv.at[part * sub_count + owner],
+                device_id=there,
+                device_id_type=MESH,
+            )
+
+        def arrived(part, owner):
+            block_ref = out_ref.at[part * sub_count + owner]
+            remote(block_ref, part, owner, core_send.at[0], (leaf, other)).wait_recv()
+
+        started = []
+
+        def start(copy):
+            copy.start()
+            started.append(copy)
+
+        def spread(part, source):
+            for k in range(1, chips):
+                there = lax.rem(chip + k, chips) * 2 + core
+                start(remote(source, part, sub, chip_send.at[part * chips + k], (leaf, there)))
+            start(remote(source, part, sub, core_send.at[part * chips], (leaf, other)))
+
+        for j, (dl, part) in enumerate(((1, 0), (leaves - 1, 2))):
+            there = lax.rem(leaf + dl, leaf_count)
+            start(remote(x_ref, part, sub, halo_send.at[j], (there, sub)))
+        spread(1, x_ref)
+        out_ref[sub_count + sub] = x_ref[...]
+
+        def forward(part):
+            for k in range(1, chips):
+                owner = lax.rem(chip + chips - k, chips) * 2 + core
+                arrived(part, owner)
+                start(
+                    remote(
+                        out_ref.at[part * sub_count + owner],
+                        part,
+                        owner,
+                        core_send.at[part * chips + k],
+                        (leaf, other),
+                    )
+                )
+
+        for part in (0, 2):
+            arrived(part, sub)
+            spread(part, out_ref.at[part * sub_count + sub])
+        for part in (1, 0, 2):
+            forward(part)
+        for part in range(3):
+            for k in range(chips):
+                arrived(part, lax.rem(chip + k, chips) * 2 + 1 - core)
+        for copy in started:
+            copy.wait_send()
+
+    return pl.pallas_call(
+        kernel,
+        out_shape=jax.ShapeDtypeStruct((3 * subs,) + block.shape, block.dtype),
+        in_specs=[VMEM],
+        out_specs=VMEM,
+        scratch_shapes=[
+            pltpu.SemaphoreType.DMA((2,)),
+            pltpu.SemaphoreType.DMA((3 * subs,)),
+            pltpu.SemaphoreType.DMA((3 * chips,)),
+            pltpu.SemaphoreType.DMA((3 * chips,)),
+        ],
+        compiler_params=pltpu.CompilerParams(
+            collective_id=collective_id, has_side_effects=True, vmem_limit_bytes=24 * 1024 * 1024
+        ),
+        name="gather_window",
+    )(block)
 
 
 def split3(x):
@@ -128,15 +325,39 @@
     leaf_count = lax.axis_size("leaf")
     leaf_index = lax.axis_index("leaf")
     own_points = points.reshape(per_device, leaf_size, feat_count)
-    skel_points = jnp.take_along_axis(own_points, skeleton[:, :, None], axis=1)
-    skel_sq = jnp.sum(skel_points * skel_points, axis=-1)
-    leaf_data = jnp.concatenate([own_points, skel_points], axis=1).transpose(0, 2, 1)
-    subtree_data = lax.all_gather(leaf_data, "sub", axis=0, tiled=True)
-    window_data = with_halo(subtree_data, (("leaf", 0),), sub_leaves)
-    window_t = window_data[:, :, :leaf_size]
+    own_t = own_points.transpose(0, 2, 1)
+    window_t = gather_window(own_t, 1).reshape(3 * sub_leaves, feat_count, leaf_size)
     scale = 1.4426950408889634 / feat_count
     targets = target_rows(own_points, scale)
-    far_points = window_data[:, :, leaf_size:][far_list].transpose(0, 1, 3, 2)
+
+    def pick(points_t, index):
+        chosen = index[..., None, :] == jnp.arange(leaf_size, dtype=jnp.int32)[:, None]
+        return jnp.einsum(
+            "...fn,...nk->...kf", points_t, chosen.astype(jnp.float32), precision=HIGHEST_PREC
+        )
+
+    lanes = 128
+    rows = sub_leaves * leaf_size // lanes
+    in_row = point_order[:, None] // lanes == jnp.arange(rows, dtype=jnp.int32)[None, :]
+    in_lane = point_order[:, None] % lanes == jnp.arange(lanes, dtype=jnp.int32)[None, :]
+    in_row, in_lane = in_row.astype(jnp.float32), in_lane.astype(jnp.float32)
+    own_rows = per_device * leaf_size // lanes
+    user_subtree, slot_index = exchange(
+        [
+            Channel(current.reshape(own_rows, lanes), (sub_count,), sub_peers(), sub_slot),
+            Channel(
+                skeleton.astype(jnp.float32), (3 * sub_count,), window_peers(), window_slot
+            ),
+        ],
+        2,
+    )
+    window_skel = slot_index.reshape(3 * sub_leaves, skel_count).astype(jnp.int32)
+    picked = jnp.dot(in_row, user_subtree.reshape(rows, lanes), precision=HIGHEST_PREC)
+    tree_vector = jnp.sum(picked * in_lane, axis=1)
+
+    skel_points = pick(own_t, skeleton)
+    skel_sq = jnp.sum(skel_points * skel_points, axis=-1)
+    far_points = pick(window_t[far_list], window_skel[far_list])
     far_inner = jnp.einsum("bmf,bjnf->bjmn", skel_points, far_points, precision=HIGHEST_PREC)
     far_kernel = gaussian(
         far_inner,
@@ -144,12 +365,11 @@
         jnp.sum(far_points * far_points, axis=-1)[:, :, None, :],
         feat_count,
     )
-    subtree_points = subtree_data[:, :, :leaf_size]
+    subtree_points = window_t[sub_leaves : 2 * sub_leaves]
     root_index = root_skeleton[0]
     own_root = subtree_points[root_index // leaf_size, :, root_index % leaf_size]
-    all_roots = lax.all_gather(own_root[None], "leaf", axis=0, tiled=True).reshape(
-        leaf_count * skel_count, feat_count
-    )
+    (all_roots_t,) = exchange([Channel(own_root.T, (leaf_count,), leaf_peers(), leaf_slot)], 3)
+    all_roots = all_roots_t.transpose(0, 2, 1).reshape(leaf_count * skel_count, feat_count)
     own_root_sq = jnp.sum(own_root * own_root, axis=-1)
     all_root_sq = jnp.sum(all_roots * all_roots, axis=-1)
     top_inner = jnp.dot(own_root, all_roots.T, precision=HIGHEST_PREC)
@@ -162,10 +382,15 @@
         skel_weights = jnp.einsum("bkn,bn->bk", leaf_maps, values, precision=HIGHEST_PREC)
         root_part = jnp.einsum("bkn,bn->k", root_maps, values, precision=HIGHEST_PREC)
         packed = jnp.concatenate([values, skel_weights], axis=1)
-        subtree_values = lax.all_gather(packed, "sub", axis=0, tiled=True)
-        window_values = with_halo(subtree_values, (("leaf", 0),), sub_leaves)
-        root_total = lax.psum(root_part, "sub")
-        root_weights = lax.all_gather(root_total[None], "leaf", axis=0, tiled=True)
+        window_values, root_parts = exchange(
+            [
+                Channel(packed, (3 * sub_count,), window_peers(), window_slot),
+                Channel(root_part[None], (leaf_count * sub_count,), all_peers(), all_slot),
+            ],
+            4,
+        )
+        window_values = window_values.reshape(3 * sub_leaves, leaf_size + skel_count)
+        root_weights = jnp.sum(root_parts.reshape(leaf_count, sub_count, skel_count), axis=1)
         window_entries = window_values[:, :leaf_size]
 
         result = near_apply(near_list, targets, window_t, window_entries[:, None, :], scale)
@@ -180,18 +405,28 @@
         result = result + jnp.einsum("bkn,k->bn", root_maps, root_out, precision=HIGHEST_PREC)
         return result.reshape(-1) + RIDGE_SHIFT * vector
 
-    user_subtree = lax.all_gather(current, "sub", axis=0, tiled=True)
-    tree_vector = jnp.take(user_subtree, point_order, axis=0)
     first_section = tree_vector - operator(tree_vector) / ritz_roots[0]
     second = first_section - operator(first_section) / ritz_roots[1]
     preconditioned = tree_vector - second
-    placed = jnp.zeros((sub_leaves * leaf_size,), jnp.float32).at[point_order].set(preconditioned)
-    user_grown = lax.psum_scatter(placed, "sub", scatter_dimension=0, tiled=True)
+    placed = jnp.einsum(
+        "ir,il->rl", in_row, preconditioned[:, None] * in_lane, precision=HIGHEST_PREC
+    ).reshape(sub_count, own_rows, lanes)
+    (pieces,) = exchange([Channel(placed, (sub_count,), sub_peers(), sub_slot, True)], 5)
+    user_grown = jnp.sum(pieces, axis=0).reshape(-1)
     local_proj = jnp.dot(krylov_basis, user_grown, precision=HIGHEST_PREC)
     local_gram = jnp.dot(krylov_basis, krylov_basis.T, precision=HIGHEST_PREC)
-    projections, squares, gram_matrix = lax.psum(
-        (local_proj, jnp.sum(user_grown * user_grown), local_gram), ("leaf", "sub")
-    )
+    basis_count = local_proj.shape[0]
+    square = jnp.sum(user_grown * user_grown)
+    totals = jnp.concatenate([local_proj, square[None], local_gram.reshape(-1)])
+    width = -(-totals.shape[0] // lanes) * lanes
+    totals = jnp.pad(totals, (0, width - totals.shape[0]))
+    (every,) = exchange(
+        [Channel(totals[None], (leaf_count * sub_count,), all_peers(), all_slot)], 6
+    )
+    totals = jnp.sum(every, axis=(0, 1))
+    projections, squares = totals[:basis_count], totals[basis_count]
+    gram_matrix = totals[basis_count + 1 : basis_count + 1 + basis_count * basis_count]
+    gram_matrix = gram_matrix.reshape(basis_count, basis_count)
     orthogonal = user_grown - jnp.dot(projections, krylov_basis, precision=HIGHEST_PREC)
     length_sq = (
         squares

time: 442 us -> 282 us (0.64)
  blocking collectives: 231 us -> 0 us
  Pallas kernels: 88.8 us -> 194 us
  local copies, waits for them, and re-layouts: 63.9 us -> 33.9 us
  between operations: 17.1 us -> 3.09 us
  matrix products: 17.8 us -> 29.2 us
  starting transfers between devices: 8.96 us -> 0 us
    all_gather x6 -> x0, blocking collectives: 165 us -> none  [the longest x2 117 us: operator(): root_weights = lax.all_gather(root_total[None], 'leaf', axis=0, tiled=True)]
    pallas_call x0 -> x7, Pallas kernels: none -> 105 us  [the longest x6 62.7 us: exchange(): pl.pallas_call(kernel, out_shape=[channel.out for channel in channels], i...]
    psum x3 -> x0, blocking collectives: 55.3 us -> none  [the longest x1 43.4 us: shards(): lax.psum((local_proj, jnp.sum(user_grown * user_grown), local_gram), ('le...]
    gather x4 -> x2, local copies, waits for them, and re-layouts: 17.6 us -> 5.38 us  [shards(): far_points = pick(window_t[far_list], window_skel[far_list])]
    unnamed x1 -> x0, blocking collectives: 10.3 us -> none
    ppermute x6 -> x0, starting transfers between devices: 8.92 us -> none  [the longest x3 6.73 us: with_halo(): lax.ppermute(lax.slice_in_dim(block, 0, width, axis=dim), axis, backward)]
    dot_general x0 -> x4, matrix products: none -> 8.33 us  [the longest x2 4.52 us: pick(): jnp.einsum('...fn,...nk->...kf', points_t, chosen.astype(jnp.float32), pr...]
    scatter x1 -> x0, local copies, waits for them, and re-layouts: 8.22 us -> none  [shards(): jnp.zeros((sub_leaves * leaf_size,), jnp.float32).at[point_order]]
  transfers between devices with their start and end apart: 7 -> 0, of which waited for: 0 -> 0; matrix products, arithmetic and copies ran while one was open for 12% -> 0% of each run, Pallas kernels for 0% -> 0%
where the time goes in v2:
time: 282 us; the launch traced here: 277 us
  Pallas kernels  194 us (69%)
  local copies, waits for them, and re-layouts  33.9 us (12%)
  matrix products  29.2 us (10%)
  other arithmetic  17 us (6%)
  between operations  3.09 us (1%)
    pallas_call x2, Pallas kernels, near_apply(): pl.pallas_call(lambda *refs: near_kernel(scale, *refs), out_shape=jax.Sha...  89.2 us
    pallas_call x6, Pallas kernels, exchange(): pl.pallas_call(kernel, out_shape=[channel.out for channel in channels], i...  62.7 us
    pallas_call x1, Pallas kernels, gather_window(): pl.pallas_call(kernel, out_shape=jax.ShapeDtypeStruct((3 * subs,) + block...  42.4 us
    concatenate x2, local copies, waits for them, and re-layouts, target_rows(): return jnp.concatenate([hi, lo, hi, one, one, one, a, b, c, pad], axis=-1)  6.21 us

profile of v2, /device:TPU:12, one launch (start us, length us, event | category | flops | bytes accessed | tf_op | source)
XLA Modules:
  0.0 277.5 jit_solution(9344622025261126473)
XLA Ops:
  0.6 1.2 fusion.58
  1.9 1.3 convert_element_type.98.refs_1_
  3.2 7.1 %exchange.6 = (f32[4,16,128]{2,1,0:T(8,128)}, f32[12,4,128]{2,1,0:T(4,128)}) custom-call(f32[16,128]{1,0:T(8,128)} %bitcast.225, f32[4,128]{1,0:T(4,128)} %convert_element_type.98.refs_1_), custom_call_target="tpu_custom_call" | custom-call | tf_op jit(solution)/shard_map/exchange/pallas_call | solution.py:92
  10.3 0.7 add_select_fusion.1
  11.0 2.0 fusion.7
  13.1 1.4 copy.34
  14.5 1.1 subtract_convert_fusion.1
  16.1 1.4 copy.35
  17.4 1.3 copy.36
  18.7 2.7 subtract_convert_fusion
  21.4 0.9 concatenate.21
  22.3 0.9 broadcast_in_dim.20
  23.2 5.4 %concatenate.22.refs_1_ = bf16[4,512,256]{2,1,0:T(8,128)(2,1)S(1)} concatenate(bf16[4,512,64]{2,1,0:T(8,128)(2,1)S(1)} %get-tuple-element.17, bf16[4,512,64]{2,1,0:T(8,128)(2,1)} %get-tuple-element.16, bf16[4,512,64]{2,1,0:T(8,128)(2,1)S(1)} %get-tuple-element.17, bf16[4,512,3]{2,1,0:T(8,128)(2,1)} %concatenate.21, bf16[4,512,1]{2,1,0:T(8,128)(2,1)S(1)} %copy.37, ...), dimensions={2} | concatenate | bytes 2097152 | tf_op jit(solution)/shard_map/concatenate | solution.py:241
  28.5 1.5 copy.38.x_ref
  30.1 42.4 %gather_window.1 = f32[12,4,64,512]{3,2,1,0:T(8,128)S(1)} custom-call(f32[4,64,512]{2,1,0:T(8,128)S(1)} %copy.38.x_ref), custom_call_target="tpu_custom_call" | custom-call | tf_op jit(solution)/shard_map/gather_window/pallas_call | solution.py:206
  72.5 2.7 copy-done.1
  75.1 1.5 slice.35
  76.7 3.9 %copy.40 = f32[16,64,512]{1,2,0:T(8,128)} copy(f32[16,64,512]{2,1,0:T(8,128)} %bitcast.203) | data formatting | bytes 4194304 | tf_op jit(solution)/shard_map/slice | solution.py:368
  80.6 1.8 gather_fusion.3
  83.1 22.2 %exchange.8 = f32[8,64,128]{2,1,0:T(8,128)} custom-call(f32[64,128]{1,0:T(8,128)} %bitcast.210), custom_call_target="tpu_custom_call" | custom-call | tf_op jit(solution)/shard_map/exchange/pallas_call | solution.py:92
  105.3 1.0 fusion.28
  106.4 2.5 fusion.12
  108.8 1.0 fusion.53
  110.4 1.4 convolution_bitcast_fusion.3.refs_1_
  111.9 9.4 %exchange.7 = (f32[12,4,640]{2,1,0:T(4,128)}, f32[32,1,128]{2,1,0:T(1,128)}) custom-call(f32[4,640]{1,0:T(4,128)} %pad_maximum_fusion.refs_0_, f32[1,128]{1,0:T(1,128)} %convolution_bitcast_fusion.3.refs_1_), custom_call_target="tpu_custom_call" | custom-call | tf_op jit(solution)/shard_map/exchange/pallas_call | solution.py:92
  121.3 0.7 reduce_sum.124
  122.0 1.6 convolution_bitcast_fusion.7
  124.2 1.0 reshape.293
  125.3 44.6 %near.2 = f32[4,512,128]{2,1,0:T(8,128)S(1)} custom-call(s32[4,32]{1,0:T(4,128)S(1)} %copy-done.2, bf16[4,512,256]{2,1,0:T(8,128)(2,1)S(1)} %concatenate.22.refs_1_, f32[48,64,512]{2,1,0:T(8,128)} %bitcast.198, f32[48,1,512]{2,1,0:T(1,128)S(1)} %broadcast_in_dim.22.refs_3_), custom_call_target="tpu_custom_call" | custom-call | tf_op jit(solution)/shard_map/near/pallas_call | solution.py:289
  170.3 4.8 %gather_fusion.1 = f32[16,64,512]{2,1,0:T(8,128)} fusion(f32[48,64,512]{2,1,0:T(8,128)} %bitcast.199, s32[1024]{0:T(1024)S(1)} %pad_clamp_fusion), kind=kCustom, calls=%fused_computation.1 | custom fusion | bytes 4194368 | tf_op jit(solution)/shard_map/gather | solution.py:360
  175.7 3.5 %multiply_reduce_fusion = (f32[4,4,128]{2,1,0:T(4,128)S(1)}, f32[4,4,128,64]{2,3,1,0:T(8,128)S(1)}) fusion(f32[4,4,64,512]{3,2,1,0:T(8,128)} %bitcast.204, s32[4,4,128]{2,1,0:T(4,128)S(1)} %bitcast.212), kind=kOutput, calls=%fused_computation.43 | convolution fusion | flops 806615040 | bytes 2637824 | tf_op jit(solution)/shard_map/...fn,...nk->...kf/dot_general | solution.py:335
  179.2 1.1 multiply_reduce_fusion.2
  180.2 3.0 %fusion.6 = f32[4,4,128,128]{2,3,1,0:T(8,128)} fusion(f32[4,4,128,64]{2,3,1,0:T(8,128)S(1)} %get-tuple-element.27, f32[4,4,128]{2,1,0:T(4,128)S(1)} %get-tuple-element.26, f32[4,128]{1,0:T(4,128)S(1)} %get-tuple-element.28, f32[4,128,64]{1,2,0:T(8,128)S(1)} %get-tuple-element.29), kind=kOutput, calls=%fused_computation.14 | convolution fusion | flops 202637312 | bytes 1714176 | tf_op jit(solution)/shard_map/bmf,bjnf->bjmn/dot_general | solution.py:361
  183.9 1.9 convolution_bitcast_fusion.1
  187.6 1.0 fusion.34
  189.2 1.5 convolution_bitcast_fusion.2.refs_1_
  190.7 9.9 %exchange.9 = (f32[12,4,640]{2,1,0:T(4,128)}, f32[32,1,128]{2,1,0:T(1,128)}) custom-call(f32[4,640]{1,0:T(4,128)} %pad_maximum_fusion.1.refs_0_, f32[1,128]{1,0:T(1,128)} %convolution_bitcast_fusion.2.refs_1_), custom_call_target="tpu_custom_call" | custom-call | tf_op jit(solution)/shard_map/exchange/pallas_call | solution.py:92
  200.6 0.9 reshape.298
  201.7 44.6 %near.3 = f32[4,512,128]{2,1,0:T(8,128)S(1)} custom-call(s32[4,32]{1,0:T(4,128)S(1)} %copy-done.2, bf16[4,512,256]{2,1,0:T(8,128)(2,1)S(1)} %concatenate.22.refs_1_, f32[48,64,512]{2,1,0:T(8,128)} %bitcast.200, f32[48,1,512]{2,1,0:T(1,128)S(1)} %broadcast_in_dim.26.refs_3_), custom_call_target="tpu_custom_call" | custom-call | tf_op jit(solution)/shard_map/near/pallas_call | solution.py:289
  246.8 1.6 convolution_bitcast_fusion.6
  251.0 1.3 subtract_subtract_fusion
  252.3 1.8 fusion.14
  254.1 5.1 %exchange.10 = f32[4,16,128]{2,1,0:T(8,128)} custom-call(f32[4,16,128]{2,1,0:T(8,128)} %bitcast.216), custom_call_target="tpu_custom_call" | custom-call | tf_op jit(solution)/shard_map/exchange/pallas_call | solution.py:92
  259.2 0.8 reduce_sum.127
  260.7 1.3 fusion.42.refs_0_
  262.0 9.1 %exchange.11 = f32[32,1,128]{2,1,0:T(1,128)} custom-call(f32[1,128]{1,0:T(1,128)} %fusion.42.refs_0_), custom_call_target="tpu_custom_call" | custom-call | tf_op jit(solution)/shard_map/exchange/pallas_call | solution.py:92
  271.1 0.8 reduce_sum.129
  275.5 0.7 fusion.18
  (84 shorter events, 13.5 us)
Async XLA Ops:
  0.6 108.2 %copy-start = (f32[4,128,512]{2,1,0:T(8,128)S(1)}, f32[4,128,512]{2,1,0:T(8,128)}, u32[]{:S(2)}) copy-start(f32[4,128,512]{2,1,0:T(8,128)} %param.12) | copy-start | bytes 3145732
  13.0 2.6 copy-start.9
  14.5 2.9 %copy-start.6 = (f32[2048,64]{1,0:T(8,128)}, f32[2048,64]{1,0:T(8,128)S(1)}, u32[]{:S(2)}) copy-start(f32[2048,64]{1,0:T(8,128)S(1)} %copy.34) | copy-start | bytes 1572868
  72.5 2.7 copy-start.1
  76.7 3.9 %copy-start.16 = (s32[1,128]{1,0:T(1,128)S(1)}, s32[1,128]{1,0:T(1,128)}, u32[]{:S(2)}) copy-start(s32[1,128]{1,0:T(1,128)} %param.19) | copy-start | bytes 1540
  80.5 29.9 %copy-start.3 = (f32[4,128,512]{2,1,0:T(8,128)S(1)}, f32[4,128,512]{2,1,0:T(8,128)}, u32[]{:S(2)}) copy-start(f32[4,128,512]{2,1,0:T(8,128)} %param.13) | copy-start | bytes 3145732
  108.8 16.4 %copy-start.2 = (s32[4,32]{1,0:T(4,128)S(1)}, s32[4,32]{1,0:T(4,128)}, u32[]{:S(2)}) copy-start(s32[4,32]{1,0:T(4,128)} %refs_0_.3) | copy-start | bytes 1540
  125.2 44.9 %copy-start.14 = (s32[4,4]{1,0:T(4,128)S(1)}, s32[4,4]{1,0:T(4,128)}, u32[]{:S(2)}) copy-start(s32[4,4]{1,0:T(4,128)} %param.21) | copy-start | bytes 196
  170.3 4.8 %copy-start.11 = (f32[12,4,128]{2,1,0:T(4,128)S(1)}, f32[12,4,128]{2,1,0:T(4,128)}, u32[]{:S(2)}) copy-start(f32[12,4,128]{2,1,0:T(4,128)} %get-tuple-element.10) | copy-start | bytes 73732
  175.1 4.0 %copy-start.7 = (f32[2048,64]{1,0:T(8,128)S(1)}, f32[2048,64]{1,0:T(8,128)}, u32[]{:S(2)}) copy-start(f32[2048,64]{1,0:T(8,128)} %copy-done.6) | copy-start | bytes 1572868
  175.1 4.0 %copy-start.13 = (s32[4,128]{1,0:T(4,128)S(1)}, s32[4,128]{1,0:T(4,128)}, u32[]{:S(2)}) copy-start(s32[4,128]{1,0:T(4,128)} %param.18) | copy-start | bytes 6148
  180.2 6.1 %copy-start.15 = (f32[2]{0:T(128)S(1)}, f32[2]{0:T(128)}, u32[]{:S(2)}) copy-start(f32[2]{0:T(128)} %param.16) | copy-start | bytes 28
  183.3 5.9 %copy-start.4 = (f32[4,128,512]{2,1,0:T(8,128)S(1)}, f32[4,128,512]{2,1,0:T(8,128)}, u32[]{:S(2)}) copy-start(f32[4,128,512]{2,1,0:T(8,128)} %param.13) | copy-start | bytes 3145732
  201.7 45.0 %copy-start.12 = (f32[32,1,128]{2,1,0:T(1,128)S(1)}, f32[32,1,128]{2,1,0:T(1,128)}, u32[]{:S(2)}) copy-start(f32[32,1,128]{2,1,0:T(1,128)} %get-tuple-element.13) | copy-start | bytes 49156
  246.3 2.0 copy-start.5
  246.7 2.9 %copy-start.8 = (f32[4,4,128,128]{2,3,1,0:T(8,128)S(1)}, f32[4,4,128,128]{2,3,1,0:T(8,128)}, u32[]{:S(2)}) copy-start(f32[4,4,128,128]{2,3,1,0:T(8,128)} %fusion.6) | copy-start | bytes 3145732
  249.0 11.5 %copy-start.10 = (f32[8,2048]{1,0:T(8,128)S(1)}, f32[8,2048]{1,0:T(8,128)}, u32[]{:S(2)}) copy-start(f32[8,2048]{1,0:T(8,128)} %param.15) | copy-start | bytes 196612
